TPU v7x, 512 devices: a whole 4x4x16 slice. The times are simulated.
512 devices in a mesh: dp: 32 (over y, x, core), tensor: 16 (over z).
Axes of the slice: x: 4, y: 4, z: 16, core: 2. Of those that a mesh axis runs over, the one named last changes fastest.
Arguments:
- hidden: bfloat16 [24576, 4096], P('dp', 'tensor'), may hold values from -4 to 4
- queries: bfloat16 [24576, 4096], P('dp', 'tensor')
- database: bfloat16 [1024, 128, 896], P('dp', 'tensor'), may hold values from -6 to 6
- w_key: bfloat16 [896, 4096], P(None, 'tensor'), may hold values from -0.1875 to 0.1875
- w_value: bfloat16 [896, 4096], P(None, 'tensor'), may hold values from -0.1875 to 0.1875
- w_out: bfloat16 [4096, 4096], P(None, 'tensor'), may hold values from -0.09375 to 0.09375
- owners: int32 [384, 2], P('dp'), may hold values from 0 to 31, all different within a row; in each aligned block of 12 rows (0 to 11, 12 to 23, ...) at most 2 rows name the same one
- entry_slots: int32 [384, 2], P('dp'), may hold values from 0 to 31
Outputs:
- mixed: bfloat16 [24576, 4096], P('dp', 'tensor')
Inputs may be any that keep to these rules, and one draw needn't show every extreme that they name: Among the spans of one dp index (aligned blocks of 12 rows) no owner is named more than 2 times, a bound that some block reaches; the 2 neighbours of a span have different owners.
All inputs are finite; a program needn't handle non-finite values.
Results may differ from a plain program's by a relative error of at most 0.012.
The roundings to bfloat16 on the way count: a program that leaves them out, or rounds other values in their place, can miss the bound.
Values may be sent and summed in bfloat16 or wider, within the bound.
A program may use at most 64 MiB of HBM per device.

v0:
```python
import math
import jax
import jax.numpy as jnp
from jax import lax
from jax.sharding import PartitionSpec as P

HEAD_DIM = 128


def per_device(hidden, queries, database, w_key, w_value, w_out, owners, entry_slots):
    dp_size = lax.axis_size("dp")
    span_count = owners.shape[0]
    per_span = owners.shape[1]
    capacity = max(2, (per_span * span_count + dp_size - 1) // dp_size)
    wanted = owners.reshape(-1)
    local_slot = entry_slots.reshape(-1)
    requests_here = wanted.shape[0]
    same_owner = wanted[:, None] == wanted[None, :]
    before = jnp.arange(requests_here)[None, :] < jnp.arange(requests_here)[:, None]
    order_in = jnp.sum(jnp.where(same_owner & before, 1, 0), axis=1).astype(jnp.int32)
    position = wanted * capacity + order_in
    placed = position[:, None] == jnp.arange(dp_size * capacity, dtype=jnp.int32)[None, :]
    request_table = jnp.sum(jnp.where(placed, (local_slot + 1)[:, None], 0), axis=0)
    request_table = request_table.reshape(dp_size, capacity)
    incoming = lax.all_to_all(request_table, "dp", split_axis=0, concat_axis=0, tiled=True)
    served_rows = jnp.maximum(incoming - 1, 0).reshape(-1)
    served = jnp.take(database, served_rows, axis=0)
    served = served.reshape(dp_size, capacity, database.shape[1], database.shape[2])
    replies = lax.all_to_all(served, "dp", split_axis=0, concat_axis=0, tiled=True)
    reply_rows = replies.reshape(dp_size * capacity, database.shape[1] * database.shape[2])
    fetched = jnp.dot(
        placed.astype(jnp.bfloat16), reply_rows, preferred_element_type=jnp.float32
    ).astype(jnp.bfloat16)
    fetched = fetched.reshape(requests_here, database.shape[1], database.shape[2])
    proj_weight = jnp.concatenate([w_key, w_value], axis=1)
    piece = lax.all_gather(fetched, "tensor", axis=1, tiled=True)
    flat_piece = piece.reshape(piece.shape[0] * piece.shape[1], piece.shape[2])
    result = jnp.dot(flat_piece, proj_weight, preferred_element_type=jnp.float32).astype(
        jnp.bfloat16
    )
    key_value = result.reshape(piece.shape[0], piece.shape[1], proj_weight.shape[1])
    width = w_key.shape[1]
    heads_here = width // HEAD_DIM
    key_value = key_value.reshape(
        span_count, per_span * key_value.shape[1], 2, heads_here, HEAD_DIM
    )
    key_rows = key_value[:, :, 0]
    value_rows = key_value[:, :, 1]
    span_size = queries.shape[0] // span_count
    query_rows = queries.reshape(span_count, span_size, heads_here, HEAD_DIM)
    score_scale = 1.0 / math.sqrt(HEAD_DIM)
    scores = (
        jnp.einsum("cihd,cjhd->chij", query_rows, key_rows, preferred_element_type=jnp.float32)
        * score_scale
    )
    row_max = jnp.max(scores, axis=-1, keepdims=True)
    weights = jnp.exp(scores - row_max)
    weights = weights / jnp.sum(weights, axis=-1, keepdims=True)
    softmax_low = weights.astype(jnp.bfloat16)
    attended = jnp.einsum(
        "chij,cjhd->cihd", softmax_low, value_rows, preferred_element_type=jnp.float32
    )
    attended = attended.astype(jnp.bfloat16).reshape(queries.shape[0], width)
    gathered = lax.all_gather(attended, "tensor", axis=1, tiled=True)
    projected = jnp.dot(gathered, w_out, preferred_element_type=jnp.float32)
    return (hidden.astype(jnp.float32) + projected).astype(jnp.bfloat16)


def solution(mesh):
    in_specs = (
        P("dp", "tensor"),
        P("dp", "tensor"),
        P("dp", "tensor", None),
        P(None, "tensor"),
        P(None, "tensor"),
        P(None, "tensor"),
        P("dp", None),
        P("dp", None),
    )
    out_specs = P("dp", "tensor")
    return jax.shard_map(
        per_device, mesh=mesh, in_specs=in_specs, out_specs=out_specs, check_vma=False
    )
```

profile of v0, /device:TPU:32, one launch (start us, length us, event | category | flops | bytes accessed | tf_op | source)
XLA Modules:
  0.0 276.5 jit_solution(5320684096094378514)
XLA Ops:
  6.5 0.9 copy.42
  7.5 0.1 reshape.77
  7.5 0.2 select_reduce_fusion.1
  7.7 0.7 broadcast_add_fusion
  8.4 0.1 copy.43
  8.5 0.1 add.43
  8.6 0.1 select_reduce_fusion
  8.7 0.1 all_to_all.9
  8.8 14.5 %all_to_all.14 = s32[32,1,2]{2,1,0:T(1,128)S(1)} all-to-all(s32[32,1,2]{2,1,0:T(1,128)S(1)} %bitcast.54), channel_id=1, replica_groups=mesh['dp'=32,'tensor'=16] {'dp'}, dimensions={0} | all-to-all | bytes 512 | tf_op jit(solution)/shard_map/all_to_all | solution.py:25
  23.3 0.1 copy.45
  23.4 0.1 copy.47
  23.5 0.1 reshape.85
  23.6 0.1 copy.46
  23.7 1.7 gather_fusion
  25.4 0.2 broadcast_select_fusion
  25.6 19.2 %all_to_all.15 = bf16[32,2,8,896]{3,2,1,0:T(8,128)(2,1)S(1)} all-to-all(bf16[32,2,8,896]{3,2,1,0:T(8,128)(2,1)S(1)} %broadcast_select_fusion), channel_id=1, replica_groups=mesh['dp'=32,'tensor'=16] {'dp'}, dimensions={0} | all-to-all | bytes 1835008 | tf_op jit(solution)/shard_map/all_to_all | solution.py:29
  44.8 0.1 copy.54
  45.0 0.3 convolution_convert_fusion
  45.3 0.8 copy.55
  46.2 0.1 reshape.81
  46.3 82.7 %all-gather.3.cloned.1.call-done = bf16[24,128,896]{2,1,0:T(8,128)(2,1)} async-done(((bf16[24,8,896]{2,1,0:T(8,128)(2,1)}), bf16[24,128,896]{2,1,0:T(8,128)(2,1)}) %all-gather.3.cloned.1.call-update) | async-done | bytes 5505040 | tf_op jit(solution)/shard_map/all_gather | solution.py:36
  128.9 7.7 %convolution_convert_fusion.1 = bf16[3072,512]{1,0:T(8,128)(2,1)} fusion(bf16[3072,896]{1,0:T(8,128)(2,1)} %bitcast.55, bf16[896,256]{1,0:T(8,128)(2,1)S(1)} %copy-done.3, bf16[896,256]{1,0:T(8,128)(2,1)} %param.11), kind=kOutput, calls=%fused_computation.3 | convolution fusion | flops 2821980160 | bytes 9568256 | tf_op jit(solution)/shard_map/dot_general | solution.py:38
  136.7 5.5 %reshape_reshape.3 = bf16[12,256,2,2,128]{4,3,2,1,0:T(2,128)(2,1)} reshape(bf16[3072,512]{1,0:T(8,128)(2,1)} %convolution_convert_fusion.1) | data formatting | bytes 6291456 | tf_op jit(solution)/shard_map/reshape;reshape | solution.py:44
  142.2 4.8 %fusion.25 = (bf16[12,256,1,2,128]{4,3,2,1,0:T(2,128)(2,1)S(1)}, bf16[12,256,1,2,128]{4,3,2,1,0:T(2,128)(2,1)}) fusion(bf16[12,256,2,2,128]{4,3,2,1,0:T(2,128)(2,1)} %reshape_reshape.3), kind=kLoop, calls=%fused_computation.38 | loop fusion | bytes 6291456 | tf_op jit(solution)/shard_map/slice | solution.py:47
  147.0 0.7 fusion.5
  147.7 1.1 copy-done.1
  148.9 0.5 fusion.26
  149.4 4.6 %fusion.11 = bf16[12,64,2,128]{3,1,2,0:T(8,128)(2,1)S(1)} fusion(bf16[12,256,1,2,128]{4,3,2,1,0:T(2,128)(2,1)} %get-tuple-element.6, f32[12,2,64]{2,1,0:T(2,128)S(1)} %fusion.26, f32[12,2,256,64]{2,3,1,0:T(8,128)} %copy-done.1), kind=kOutput, calls=%fused_computation.17 | convolution fusion | flops 102041344 | bytes 3545088 | tf_op jit(solution)/shard_map/chij,cjhd->cihd/dot_general | solution.py:60
  154.0 0.4 copy.51
  154.4 0.8 copy.70
  155.3 109.1 %all-gather.5.cloned.1.call-done = bf16[768,4096]{1,0:T(8,128)(2,1)} async-done(((bf16[768,256]{1,0:T(8,128)(2,1)}), bf16[768,4096]{1,0:T(8,128)(2,1)}) %all-gather.5.cloned.1.call-update) | async-done | bytes 6291472 | tf_op jit(solution)/shard_map/all_gather | solution.py:64
  264.3 5.3 %fusion.9 = bf16[768,256]{1,0:T(8,128)(2,1)} fusion(bf16[768,4096]{1,0:T(8,128)(2,1)} %all-gather.5.cloned.1.call-done, bf16[4096,256]{1,0:T(8,128)(2,1)S(1)} %copy-done, bf16[768,256]{1,0:T(8,128)(2,1)S(1)} %copy-done.4), kind=kOutput, calls=%fused_computation.15 | convolution fusion | flops 1611202560 | bytes 9175040 | tf_op jit(solution)/shard_map/dot_general | solution.py:65
  (17 shorter events, 0.1 us)
Async XLA Ops:
  6.5 257.8 %copy-start = (bf16[4096,256]{1,0:T(8,128)(2,1)S(1)}, bf16[4096,256]{1,0:T(8,128)(2,1)}, u32[]{:S(2)}) copy-start(bf16[4096,256]{1,0:T(8,128)(2,1)} %param.13) | copy-start | bytes 6291460
  6.5 122.4 %all-gather.3.cloned.1.call-start = ((), (), s32[]{:S(2)}) async-start(), calls=%async_computation.2 | async-start | bytes 5849088 | tf_op jit(solution)/shard_map/all_gather | solution.py:36
  45.0 1.2 copy-start.2
  45.0 83.9 %copy-start.3 = (bf16[896,256]{1,0:T(8,128)(2,1)S(1)}, bf16[896,256]{1,0:T(8,128)(2,1)}, u32[]{:S(2)}) copy-start(bf16[896,256]{1,0:T(8,128)(2,1)} %param.12) | copy-start | bytes 1376260
  46.1 218.2 %all-gather.5.cloned.1.call-start = ((), (), s32[]{:S(2)}) async-start(), calls=%async_computation.3 | async-start | bytes 6684672 | tf_op jit(solution)/shard_map/all_gather | solution.py:64
  147.7 1.2 copy-start.1
  154.0 110.3 %copy-start.4 = (bf16[768,256]{1,0:T(8,128)(2,1)S(1)}, bf16[768,256]{1,0:T(8,128)(2,1)}, u32[]{:S(2)}) copy-start(bf16[768,256]{1,0:T(8,128)(2,1)} %param.8) | copy-start | bytes 1179652
Sparse Core Ops, SparseCore 0:
  46.2 82.6 all-gather.2
  155.4 108.8 all-gather.4
where the time goes:
time: 277 us; the launch traced here: 276 us
  waiting for transfers between devices  192 us (69%)
  blocking collectives  33.7 us (12%)
  matrix products  18.7 us (7%)
  local copies, waits for them, and re-layouts  17.1 us (6%)
  between operations  13.5 us (5%)
    all_gather x1, waiting for transfers between devices, per_device(): gathered = lax.all_gather(attended, 'tensor', axis=1, tiled=True)  109 us
    all_gather x1, waiting for transfers between devices, per_device(): piece = lax.all_gather(fetched, 'tensor', axis=1, tiled=True)  82.7 us
    all_to_all x1, blocking collectives, per_device(): lax.all_to_all(served, 'dp', split_axis=0, concat_axis=0, tiled=True)  19.2 us
    all_to_all x1, blocking collectives, per_device(): lax.all_to_all(request_table, 'dp', split_axis=0, concat_axis=0, tiled=True)  14.5 us
    dot_general x1, matrix products, per_device(): jnp.dot(flat_piece, proj_weight, preferred_element_type=jnp.float32)  7.74 us
  transfers between devices with their start and end apart: 2, of which 2 were waited for; matrix products, arithmetic and copies ran while one was open for 0% of the time, Pallas kernels for 0%

commit v1 on v0

--- a/solution.py
+++ b/solution.py
@@ -61,7 +61,9 @@
         "chij,cjhd->cihd", softmax_low, value_rows, preferred_element_type=jnp.float32
     )
     attended = attended.astype(jnp.bfloat16).reshape(queries.shape[0], width)
-    gathered = lax.all_gather(attended, "tensor", axis=1, tiled=True)
+    gathered = jnp.concatenate(
+        lax.all_to_all(jnp.stack([attended] * lax.axis_size("tensor")), "tensor", 0, 0), axis=1
+    )
     projected = jnp.dot(gathered, w_out, preferred_element_type=jnp.float32)
     return (hidden.astype(jnp.float32) + projected).astype(jnp.bfloat16)
 

time: 277 us -> 443 us (1.60)
  the two profiles are of different devices: /device:TPU:32 before, /device:TPU:2 now
where the time goes in v1:
time: 443 us; the launch traced here: 442 us
  blocking collectives  311 us (70%)
  waiting for transfers between devices  83.4 us (19%)
  local copies, waits for them, and re-layouts  17 us (4%)
  matrix products  15.9 us (4%)
  between operations  13.5 us (3%)
    all_to_all x1, blocking collectives, per_device(): lax.all_to_all(jnp.stack([attended] * lax.axis_size('tensor')), 'tensor',...  277 us
    all_gather x1, waiting for transfers between devices, per_device(): piece = lax.all_gather(fetched, 'tensor', axis=1, tiled=True)  83.3 us
    all_to_all x1, blocking collectives, per_device(): lax.all_to_all(served, 'dp', split_axis=0, concat_axis=0, tiled=True)  19.2 us
    all_to_all x1, blocking collectives, per_device(): lax.all_to_all(request_table, 'dp', split_axis=0, concat_axis=0, tiled=True)  14.8 us
  transfers between devices with their start and end apart: 1, of which 1 were waited for; matrix products, arithmetic and copies ran while one was open for 0% of the time, Pallas kernels for 0%

profile of v1, /device:TPU:2, one launch (start us, length us, event | category | flops | bytes accessed | tf_op | source)
XLA Modules:
  0.0 442.4 jit_solution(14204347976980766215)
XLA Ops:
  6.5 0.8 broadcast_add_fusion
  7.4 0.1 copy.46
  7.5 0.1 add.43
  7.6 0.8 copy.45
  8.3 0.1 reshape.82
  8.4 0.2 select_reduce_fusion.1
  8.6 0.1 select_reduce_fusion
  8.7 0.1 all_to_all.12
  8.8 14.8 %all_to_all.19 = s32[32,1,2]{2,1,0:T(1,128)S(1)} all-to-all(s32[32,1,2]{2,1,0:T(1,128)S(1)} %bitcast.58), channel_id=1, replica_groups=mesh['dp'=32,'tensor'=16] {'dp'}, dimensions={0} | all-to-all | bytes 512 | tf_op jit(solution)/shard_map/all_to_all | solution.py:25
  23.7 0.1 copy.49
  23.8 0.1 copy.50
  23.9 0.1 reshape.91
  24.0 1.7 gather_fusion
  25.7 0.2 broadcast_select_fusion
  25.9 19.2 %all_to_all.20 = bf16[32,2,8,896]{3,2,1,0:T(8,128)(2,1)S(1)} all-to-all(bf16[32,2,8,896]{3,2,1,0:T(8,128)(2,1)S(1)} %broadcast_select_fusion), channel_id=1, replica_groups=mesh['dp'=32,'tensor'=16] {'dp'}, dimensions={0} | all-to-all | bytes 1835008 | tf_op jit(solution)/shard_map/all_to_all | solution.py:29
  45.1 0.1 copy.58
  45.3 0.3 convolution_convert_fusion
  45.6 0.8 copy.59
  46.4 0.1 reshape.86
  46.5 83.3 %all-gather.2.cloned.1.call-done = bf16[24,128,896]{2,1,0:T(8,128)(2,1)} async-done(((bf16[24,8,896]{2,1,0:T(8,128)(2,1)}), bf16[24,128,896]{2,1,0:T(8,128)(2,1)}) %all-gather.2.cloned.1.call-update) | async-done | bytes 5505040 | tf_op jit(solution)/shard_map/all_gather | solution.py:36
  129.9 7.7 %convolution_convert_fusion.1 = bf16[3072,512]{1,0:T(8,128)(2,1)} fusion(bf16[3072,896]{1,0:T(8,128)(2,1)} %bitcast.59, bf16[896,256]{1,0:T(8,128)(2,1)S(1)} %copy-done.4, bf16[896,256]{1,0:T(8,128)(2,1)} %param.11), kind=kOutput, calls=%fused_computation.3 | convolution fusion | flops 2821980160 | bytes 9568256 | tf_op jit(solution)/shard_map/dot_general | solution.py:38
  137.6 5.5 %reshape_reshape.3 = bf16[12,256,2,2,128]{4,3,2,1,0:T(2,128)(2,1)} reshape(bf16[3072,512]{1,0:T(8,128)(2,1)} %convolution_convert_fusion.1) | data formatting | bytes 6291456 | tf_op jit(solution)/shard_map/reshape;reshape | solution.py:44
  143.1 4.8 %fusion.25 = (bf16[12,256,1,2,128]{4,3,2,1,0:T(2,128)(2,1)S(1)}, bf16[12,256,1,2,128]{4,3,2,1,0:T(2,128)(2,1)}) fusion(bf16[12,256,2,2,128]{4,3,2,1,0:T(2,128)(2,1)} %reshape_reshape.3), kind=kLoop, calls=%fused_computation.38 | loop fusion | bytes 6291456 | tf_op jit(solution)/shard_map/slice | solution.py:47
  148.0 0.7 fusion.5
  148.7 1.1 copy-done.1
  149.8 0.5 fusion.26
  150.3 4.6 %fusion.11 = bf16[12,64,2,128]{3,1,2,0:T(8,128)(2,1)S(1)} fusion(bf16[12,256,1,2,128]{4,3,2,1,0:T(2,128)(2,1)} %get-tuple-element.6, f32[12,2,64]{2,1,0:T(2,128)S(1)} %fusion.26, f32[12,2,256,64]{2,3,1,0:T(8,128)} %copy-done.1), kind=kOutput, calls=%fused_computation.17 | convolution fusion | flops 102041344 | bytes 3545088 | tf_op jit(solution)/shard_map/chij,cjhd->cihd/dot_general | solution.py:60
  155.0 0.4 copy.54
  155.4 0.2 copy.55
  155.6 0.6 stack.3
  156.3 276.8 %all_to_all.21 = bf16[16,768,256]{1,2,0:T(8,128)(2,1)S(1)} all-to-all(bf16[16,768,256]{1,2,0:T(8,128)(2,1)S(1)} %stack.3), channel_id=1, replica_groups=mesh['dp'=32,'tensor'=16] {'tensor'}, dimensions={0} | all-to-all | bytes 12582912 | tf_op jit(solution)/shard_map/all_to_all | solution.py:65
  433.0 2.6 fusion.9
  (17 shorter events, 0.2 us)
Async XLA Ops:
  6.5 426.5 %copy-start = (bf16[4096,256]{1,0:T(8,128)(2,1)S(1)}, bf16[4096,256]{1,0:T(8,128)(2,1)}, u32[]{:S(2)}) copy-start(bf16[4096,256]{1,0:T(8,128)(2,1)} %param.13) | copy-start | bytes 6291460
  6.5 123.3 %all-gather.2.cloned.1.call-start = ((), (), s32[]{:S(2)}) async-start(), calls=%async_computation.3 | async-start | bytes 5849088 | tf_op jit(solution)/shard_map/all_gather | solution.py:36
  45.3 1.1 copy-start.3
  45.3 84.6 %copy-start.4 = (bf16[896,256]{1,0:T(8,128)(2,1)S(1)}, bf16[896,256]{1,0:T(8,128)(2,1)}, u32[]{:S(2)}) copy-start(bf16[896,256]{1,0:T(8,128)(2,1)} %param.12) | copy-start | bytes 1376260
  148.7 1.2 copy-start.1
  156.2 276.8 %copy-start.2 = (bf16[768,256]{1,0:T(8,128)(2,1)S(1)}, bf16[768,256]{1,0:T(8,128)(2,1)}, u32[]{:S(2)}) copy-start(bf16[768,256]{1,0:T(8,128)(2,1)} %param.8) | copy-start | bytes 1179652
Sparse Core Ops, SparseCore 0:
  46.5 83.2 all-gather.1
